TPU v7x, 32 devices: a whole 2x2x4 slice. The times are simulated.
32 devices in a mesh: pipe: 4 (over x, core), dp: 8 (over z, y).
Axes of the slice: x: 2, y: 2, z: 4, core: 2. Of those that a mesh axis runs over, the one named last changes fastest.
Arguments:
- saved_inputs: bfloat16 [4, 4096, 896], P('pipe', 'dp'), may hold values from -6 to 6
- projections: bfloat16 [4, 896, 1792], P('pipe', 'dp'), may hold values from -0.09375 to 0.09375
- mixing: bfloat16 [4, 16, 8, 256, 256], P('pipe', 'dp'), may hold values from -0.375 to 0.375
- out_cotangent: bfloat16 [4096, 896], P('dp'), may hold values from -6 to 6
Outputs:
- section_cotangents: bfloat16 [4, 4096, 896], P('pipe', 'dp')
- weight_grads: float32 [4, 896, 1792], P('pipe', 'dp')
All inputs are finite; a program needn't handle non-finite values.
Results may differ from a plain program's by a relative error of at most 0.028.
Values may be sent and summed in bfloat16 or wider, within the bound.
A program may use at most 64 MiB of HBM per device.

v0:
```python
import functools

import jax
import jax.numpy as jnp
from jax import lax
from jax.experimental import pallas as pl
from jax.experimental.pallas import tpu as pltpu
from jax.sharding import PartitionSpec as P

FORWARD = "bhij,bjhd->bihd"
BACKWARD = "bhij,bihd->bjhd"


def from_behind(value, axis, by):
    length = lax.axis_size(axis)
    pairs = [(i, i + by) for i in range(length) if 0 <= i + by < length]
    return lax.ppermute(value, axis, pairs)


def normalize(row_block):
    widened = row_block.astype(jnp.float32)
    centred = widened - jnp.mean(widened, axis=-1, keepdims=True)
    inverse = lax.rsqrt(jnp.mean(centred * centred, axis=-1, keepdims=True) + 1e-06)
    return (centred * inverse, inverse)


def mix_heads(weights, row_block, pattern):
    images, head_count, patches = (weights.shape[0], weights.shape[1], weights.shape[2])
    per_head = row_block.reshape(images, patches, head_count, -1)
    mixed_rows = jnp.einsum(pattern, weights, per_head, preferred_element_type=jnp.float32)
    return mixed_rows.reshape(images * patches, -1).astype(jnp.bfloat16)


def norm_backward(cotangent, d_normed, scaled, inverse):
    inner = (
        d_normed
        - jnp.mean(d_normed, axis=-1, keepdims=True)
        - scaled * jnp.mean(d_normed * scaled, axis=-1, keepdims=True)
    )
    return (cotangent.astype(jnp.float32) + inverse * inner).astype(jnp.bfloat16)


def row_product(left, right):
    return lax.dot_general(
        left, right, (((0,), (0,)), ((), ())), preferred_element_type=jnp.float32
    )


def body(saved_inputs, projections, mixing, out_cotangent):
    section_count = lax.axis_size("pipe")
    section_id = lax.axis_index("pipe")
    inputs = saved_inputs[0]
    mixes = mixing[0]
    micro_count = mixes.shape[0]
    patches = mixes.shape[-1]
    width = inputs.shape[1]
    gathered = lax.all_gather(projections[0], "dp", axis=0, tiled=True)
    head_cols = gathered.shape[1] // 2
    value_weight = gathered[:, :head_cols]
    output_weight = gathered[:, head_cols:]
    total_rows = inputs.shape[0]

    def input_side(row_block, mix_block, cotangent):
        scaled, inverse = normalize(row_block)
        d_context = jnp.dot(cotangent, output_weight, preferred_element_type=jnp.float32).astype(
            jnp.bfloat16
        )
        d_values = mix_heads(mix_block, d_context, BACKWARD)
        d_normed = lax.dot_general(
            d_values, value_weight, (((1,), (1,)), ((), ())), preferred_element_type=jnp.float32
        )
        return (
            scaled.astype(jnp.bfloat16),
            d_values,
            norm_backward(cotangent, d_normed, scaled, inverse),
        )

    cot_buffer = jnp.zeros((total_rows, width), jnp.bfloat16)
    carried = (
        cot_buffer,
        jnp.zeros((total_rows, width), jnp.bfloat16),
        jnp.zeros((total_rows, width), jnp.bfloat16),
        jnp.zeros((total_rows, head_cols), jnp.bfloat16),
    )

    def active_step(holding, row_start, mix_block, cotangent):
        row_block = lax.dynamic_slice_in_dim(inputs, row_start, patches, 0)
        normed, d_values, input_grad = input_side(row_block, mix_block, cotangent)
        pieces = (input_grad, normed, cotangent, d_values)
        updated = tuple(
            (
                lax.dynamic_update_slice_in_dim(buffer, piece, row_start, 0)
                for buffer, piece in zip(holding, pieces)
            )
        )
        return (updated, input_grad)

    def advance(instant, loop_state):
        incoming, holding = loop_state
        position = instant - (section_count - 1 - section_id)
        active = jnp.logical_and(position >= 0, position < micro_count)
        clamped = jnp.clip(position, 0, micro_count - 1)
        row_start = clamped * patches
        fresh_rows = lax.dynamic_slice_in_dim(out_cotangent, row_start, patches, 0)
        cotangent = jnp.where(section_id == section_count - 1, fresh_rows, incoming)
        mix_block = lax.dynamic_slice_in_dim(mixes, clamped, 1, 0)

        def run_step(state_now):
            return active_step(state_now, row_start, mix_block, cotangent)

        def empty_step(state_now):
            return (state_now, jnp.zeros_like(cotangent))

        holding, input_grad = lax.cond(active, run_step, empty_step, holding)
        incoming = from_behind(input_grad, "pipe", -1)
        return (incoming, holding)

    start_state = (jnp.zeros((patches, width), jnp.bfloat16), carried)
    incoming, carried = lax.fori_loop(0, section_count + micro_count - 1, advance, start_state)
    section_grads, normed_all, cotangents_all, d_values_all = carried
    values_all = jnp.dot(normed_all, value_weight, preferred_element_type=jnp.float32).astype(
        jnp.bfloat16
    )
    context_all = mix_heads(mixes, values_all, FORWARD)
    weight_grads = lax.psum_scatter(
        jnp.concatenate(
            [row_product(normed_all, d_values_all), row_product(cotangents_all, context_all)],
            axis=1,
        ).astype(jnp.bfloat16),
        "dp",
        scatter_dimension=0,
        tiled=True,
    ).astype(jnp.float32)
    return (section_grads[None], weight_grads[None])


LANES = 128
MESH = pl.DeviceIdType.MESH


def ring_index(position, length):
    return jnp.where(position < length // 2, 2 * position, 2 * (length - 1 - position) + 1)


def fused_kernel(
    x_hbm, w_hbm, mix_hbm, oc_hbm, sc_hbm, wg_hbm,
    x_ref, mix_ref, sc_ref, wg_ref, sums, weights, scaled, inverse, normed, lefts, rights, mix_t, cot, d_ctx, vals, partial, landing,
    ag_send, ag_recv, rs_send, rs_recv, cot_send, cot_recv, load_sem, sc_sem, wg_sem,
):
    n = lax.axis_size("dp")
    sections = lax.axis_size("pipe")
    me = lax.axis_index("dp")
    s = lax.axis_index("pipe")
    place = jnp.where(lax.rem(me, 2) == 0, me // 2, n - 1 - me // 2)
    up = ring_index(lax.rem(place + 1, n), n)
    down = ring_index(lax.rem(place + n - 1, n), n)
    share = w_hbm.shape[0]
    width, both = weights.shape
    hd = both // 2
    images, heads, patches = mix_ref.shape[:3]
    tiles = hd // LANES
    near = (tiles + 1) // 2 * LANES
    far = hd - near

    last = s == sections - 1

    def rows_of(position):
        return pl.ds(pl.multiple_of(ring_index(position, n) * share, 16), share)

    load_w = pltpu.make_async_copy(w_hbm, weights.at[rows_of(place), :], load_sem.at[3])
    load_x = pltpu.make_async_copy(x_hbm, x_ref, load_sem.at[0])
    load_mix = pltpu.make_async_copy(mix_hbm, mix_ref, load_sem.at[1])
    load_cot = pltpu.make_async_copy(oc_hbm, cot, load_sem.at[2])

    load_w.start()
    barrier = pltpu.get_barrier_semaphore()
    for target in ({"dp": up}, {"dp": down}):
        pl.semaphore_signal(barrier, inc=1, device_id=target, device_id_type=MESH)
    for step in (1, sections - 1):
        pl.semaphore_signal(
            barrier, inc=1, device_id={"pipe": lax.rem(s + step, sections)}, device_id_type=MESH
        )
    pl.semaphore_wait(barrier, 4)

    ag_streams = []
    for direction, first, count in (
        (1, hd, near), (-1, hd + near, far), (1, 0, far), (-1, far, near)
    ):
        cut = (count // LANES + 1) // 2 * LANES
        ag_streams += [(direction, first, cut), (direction, first + cut, count - cut)]
    lanes_of = range(len(ag_streams))

    def ag_copy(k, t, arriving):
        direction, first, count = ag_streams[k]
        offset = t + 1 if arriving else t
        position = lax.rem(place - direction * offset + 2 * n, n)
        block = weights.at[rows_of(position), pl.ds(first, count)]
        return pltpu.make_async_remote_copy(
            src_ref=block, dst_ref=block,
            send_sem=ag_send.at[k, t], recv_sem=ag_recv.at[k, t],
            device_id={"dp": up if direction == 1 else down}, device_id_type=MESH,
        )

    load_w.wait()
    for k in lanes_of:
        ag_copy(k, 0, False).start()

    load_x.start()
    load_mix.start()

    @pl.when(last)
    def _():
        load_cot.start()

    def prepare_rows(u):
        rows = pl.ds(pl.multiple_of(u * LANES, LANES), LANES)
        wide = x_ref[rows, :].astype(jnp.float32)
        centred = wide - jnp.mean(wide, axis=-1, keepdims=True)
        inv = lax.rsqrt(jnp.mean(centred * centred, axis=-1, keepdims=True) + 1e-06)
        unit = centred * inv
        scaled[rows, :] = unit
        inverse[rows, :] = inv
        rounded = unit.astype(jnp.bfloat16)
        normed[rows, :] = rounded
        lefts[0, :, rows] = rounded.T

    def prepare_mix(u):
        b, h = u // heads, lax.rem(u, heads)
        mix_t[b, h] = mix_ref[b, h].T

    def prepare(t):
        for count, work in ((x_ref.shape[0] // LANES, prepare_rows), (images * heads, prepare_mix)):
            pl.loop(t * count // (n - 1), (t + 1) * count // (n - 1))(work)

    load_x.wait()
    load_mix.wait()

    @pl.when(last)
    def _():
        load_cot.wait()

    @pl.loop(0, n - 1)
    def _(t):
        for k in lanes_of:
            ag_copy(k, t, True).wait_recv()

            @pl.when(t < n - 2)
            def _():
                ag_copy(k, t + 1, False).start()

        prepare(t)

    @pl.loop(0, n - 1)
    def _(t):
        for k in lanes_of:
            ag_copy(k, t, False).wait_send()

    head_width = hd // heads
    lane = lax.broadcasted_iota(jnp.int32, (patches, LANES), 1)

    def mix_rows(matrices, b, source, dest, rows):
        made = {}
        for h in range(heads):
            low, high = h * head_width // LANES, ((h + 1) * head_width - 1) // LANES
            product = jnp.dot(
                matrices[b, h],
                source[rows, low * LANES : (high + 1) * LANES],
                preferred_element_type=jnp.float32,
            )
            for tile in range(low, high + 1):
                piece = product[:, (tile - low) * LANES : (tile - low + 1) * LANES]
                begin = h * head_width - tile * LANES
                made[tile] = piece if tile not in made else jnp.where(lane < begin, made[tile], piece)
                if (h + 1) * head_width >= (tile + 1) * LANES:
                    dest[rows, tile * LANES : (tile + 1) * LANES] = made[tile].astype(jnp.bfloat16)

    def cot_copy(b):
        rows = pl.ds(pl.multiple_of(b * patches, patches), patches)
        return pltpu.make_async_remote_copy(
            src_ref=sc_ref.at[rows, :], dst_ref=cot.at[rows, :],
            send_sem=cot_send.at[b], recv_sem=cot_recv.at[b],
            device_id={"pipe": lax.rem(s + sections - 1, sections)}, device_id_type=MESH,
        )

    d_values, context = rights.at[0], rights.at[1]

    def sc_copy(b):
        rows = pl.ds(pl.multiple_of(b * patches, patches), patches)
        return pltpu.make_async_copy(sc_ref.at[rows, :], sc_hbm.at[rows, :], sc_sem.at[b])

    def forward(b):
        rows = pl.ds(pl.multiple_of(b * patches, patches), patches)
        vals[rows, :] = jnp.dot(
            normed[rows, :], weights[:, :hd], preferred_element_type=jnp.float32
        ).astype(jnp.bfloat16)
        mix_rows(mix_ref, b, vals, context, rows)

    def to_values(b):
        rows = pl.ds(pl.multiple_of(b * patches, patches), patches)

        @pl.when(jnp.logical_not(last))
        def _():
            cot_copy(b).wait_recv()

        d_ctx[rows, :] = jnp.dot(
            cot[rows, :], weights[:, hd:], preferred_element_type=jnp.float32
        ).astype(jnp.bfloat16)
        mix_rows(mix_t, b, d_ctx, d_values, rows)

    def to_input(b):
        rows = pl.ds(pl.multiple_of(b * patches, patches), patches)
        d_normed = lax.dot_general(
            d_values[rows, :], weights[:, :hd], (((1,), (1,)), ((), ())),
            preferred_element_type=jnp.float32,
        )
        unit = scaled[rows, :]
        inner = (
            d_normed
            - jnp.mean(d_normed, axis=-1, keepdims=True)
            - unit * jnp.mean(d_normed * unit, axis=-1, keepdims=True)
        )
        sc_ref[rows, :] = (cot[rows, :].astype(jnp.float32) + inverse[rows, :] * inner).astype(jnp.bfloat16)

        @pl.when(s > 0)
        def _():
            cot_copy(b).start()

        sc_copy(b).start()

    rs_streams = []
    for direction, half, first, count in (
        (1, 0, 0, near), (-1, 1, 0, near), (1, 0, near, far), (-1, 1, near, far)
    ):
        cut = (count // LANES + 1) // 2 * LANES
        rs_streams += [
            (direction, half, first, cut), (direction, half, first + cut, count - cut)
        ]

    def wg_copy(k):
        _, half, first, count = rs_streams[k]
        columns = pl.ds(half * hd + first, count)
        return pltpu.make_async_copy(wg_ref.at[:, columns], wg_hbm.at[:, columns], wg_sem.at[k])

    def rs_copy(k, t):
        direction, half, first, count = rs_streams[k]
        columns = pl.ds(first, count)
        if isinstance(t, int):
            origin = partial.at[half, rows_of(lax.rem(place - direction + n, n)), columns]
        else:
            origin = landing.at[half, jnp.maximum(t - 1, 0), :, columns]
        return pltpu.make_async_remote_copy(
            src_ref=origin, dst_ref=landing.at[half, t, :, columns],
            send_sem=rs_send.at[k, t], recv_sem=rs_recv.at[k, t],
            device_id={"dp": up if direction == 1 else down}, device_id_type=MESH,
        )

    part = width // 2

    def gradients(b):
        rows = pl.ds(pl.multiple_of(b * patches, patches), patches)
        lefts[1, :, rows] = cot[rows, :].T

        @pl.loop(0, 4)
        def _(i):
            half = i // 2
            block = pl.ds(pl.multiple_of(lax.rem(i, 2) * part, 16), part)
            term = jnp.dot(
                lefts[half, block, rows], rights[half, rows, :],
                preferred_element_type=jnp.float32,
            )

            @pl.when(jnp.logical_and(b == 0, b < images - 1))
            def _():
                sums[half, block, :] = term

            @pl.when(jnp.logical_and(b > 0, b < images - 1))
            def _():
                sums[half, block, :] += term

            @pl.when(b == images - 1)
            def _():
                total = term if images == 1 else sums[half, block, :] + term
                partial[half, block, :] = total.astype(jnp.bfloat16)

        @pl.when(b == images - 1)
        def _():
            for k in lanes_of:
                rs_copy(k, 0).start()

    @pl.loop(0, 4 * images)
    def _(i):
        early = i < images
        after = jnp.maximum(i - images, 0)
        turn = lax.rem(after, 3)
        own = jnp.where(early, 0, jnp.where(s == 0, jnp.where(turn == 0, 1, 4 - turn), 1 + turn))
        own_b = jnp.where(early, i, after // 3)
        final = jnp.where(
            i < 2 * images, 1 + lax.rem(i, 2), jnp.where(i < 3 * images, 0, 3)
        )
        final_b = jnp.where(i < 2 * images, i // 2, lax.rem(i, images))
        work = jnp.where(last, final, own)
        b = jnp.where(last, final_b, own_b)
        for number, action in enumerate((forward, to_values, to_input, gradients)):
            pl.when(work == number)(functools.partial(action, b))

    @pl.loop(0, n - 1)
    def _(t):
        for k in lanes_of:
            direction, half, first, count = rs_streams[k]
            columns = pl.ds(first, count)
            rs_copy(k, t).wait_recv()
            position = lax.rem(place - direction * (t + 2) + 2 * n, n)
            total = landing[half, t, :, columns].astype(jnp.float32) + partial[
                half, rows_of(position), columns
            ].astype(jnp.float32)

            @pl.when(t < n - 2)
            def _():
                landing[half, t, :, columns] = total.astype(jnp.bfloat16)
                rs_copy(k, t + 1).start()

            @pl.when(t == n - 2)
            def _():
                wg_ref[:, pl.ds(half * hd + first, count)] = total
                wg_copy(k).start()

    @pl.loop(0, n - 1)
    def _(t):
        for k in lanes_of:
            rs_copy(k, t).wait_send()

    @pl.when(s > 0)
    def _():
        @pl.loop(0, images)
        def _(b):
            cot_copy(b).wait_send()

    @pl.loop(0, images)
    def _(b):
        sc_copy(b).wait()

    for k in lanes_of:
        wg_copy(k).wait()


def fused_body(saved_inputs, projections, mixing, out_cotangent):
    n = lax.axis_size("dp")
    rows, width = out_cotangent.shape
    share, both = projections.shape[1:]
    hd = both // 2
    images, heads, patches = mixing.shape[1:4]
    bf16, f32 = jnp.bfloat16, jnp.float32
    hbm = pl.BlockSpec(memory_space=pl.ANY)
    section_grads, weight_grads = pl.pallas_call(
        fused_kernel,
        out_shape=(
            jax.ShapeDtypeStruct((rows, width), bf16),
            jax.ShapeDtypeStruct((share, both), f32),
        ),
        in_specs=[hbm] * 4,
        out_specs=(hbm, hbm),
        scratch_shapes=[
            pltpu.VMEM((rows, width), bf16),
            pltpu.VMEM((images, heads, patches, patches), bf16),
            pltpu.VMEM((rows, width), bf16),
            pltpu.VMEM((share, both), f32),
            pltpu.VMEM((2, width, hd), f32),
            pltpu.VMEM((width, both), bf16),
            pltpu.VMEM((rows, width), f32),
            pltpu.VMEM((rows, 1), f32),
            pltpu.VMEM((rows, width), bf16),
            pltpu.VMEM((2, width, rows), bf16),
            pltpu.VMEM((2, rows, hd), bf16),
            pltpu.VMEM((images, heads, patches, patches), bf16),
            pltpu.VMEM((rows, width), bf16),
            pltpu.VMEM((rows, hd), bf16),
            pltpu.VMEM((rows, hd), bf16),
            pltpu.VMEM((2, width, hd), bf16),
            pltpu.VMEM((2, n - 1, share, hd), bf16),
            pltpu.SemaphoreType.DMA((8, n - 1)),
            pltpu.SemaphoreType.DMA((8, n - 1)),
            pltpu.SemaphoreType.DMA((8, n - 1)),
            pltpu.SemaphoreType.DMA((8, n - 1)),
            pltpu.SemaphoreType.DMA((images,)),
            pltpu.SemaphoreType.DMA((images,)),
            pltpu.SemaphoreType.DMA((4,)),
            pltpu.SemaphoreType.DMA((images,)),
            pltpu.SemaphoreType.DMA((8,)),
        ],
        compiler_params=pltpu.CompilerParams(
            collective_id=0, has_side_effects=True, vmem_limit_bytes=48 * 1024 * 1024
        ),
    )(*(pltpu.with_memory_space_constraint(a, pltpu.HBM) for a in (saved_inputs[0], projections[0], mixing[0], out_cotangent)))
    return (section_grads[None], weight_grads[None])


def any_body(saved_inputs, projections, mixing, out_cotangent):
    share, both = projections.shape[1:]
    width = saved_inputs.shape[2]
    n = lax.axis_size("dp")
    aligned = (
        share % 16 == 0
        and both % (2 * LANES) == 0
        and width % LANES == 0
        and mixing.shape[3] % LANES == 0
        and n % 2 == 0
        and lax.axis_size("pipe") > 2
        and lax.axis_size("pipe") % 2 == 0
    )
    chosen = fused_body if aligned else body
    return chosen(saved_inputs, projections, mixing, out_cotangent)


def solution(mesh):
    return jax.shard_map(
        any_body,
        mesh=mesh,
        in_specs=(
            P("pipe", "dp", None),
            P("pipe", "dp", None),
            P("pipe", "dp", None, None, None),
            P("dp", None),
        ),
        out_specs=(P("pipe", "dp", None), P("pipe", "dp", None)),
        check_vma=False,
    )
```

profile of v0, /device:TPU:0, one launch (start us, length us, event | category | flops | bytes accessed | tf_op | source)
XLA Modules:
  0.0 97.0 jit_solution(5182859527249581840)
XLA Ops:
  0.6 94.6 %shard_map.59 = (bf16[512,896]{1,0:T(8,128)(2,1)S(1)}, f32[112,1792]{1,0:T(8,128)S(1)}) custom-call(bf16[512,896]{1,0:T(8,128)(2,1)} %bitcast.8, bf16[112,1792]{1,0:T(8,128)(2,1)} %bitcast.9, bf16[2,8,256,256]{3,2,1,0:T(8,128)(2,1)} %bitcast.7, bf16[512,896]{1,0:T(8,128)(2,1)} %oc_hbm.1), custom_call_target="tpu_custom_call" | custom-call | tf_op jit(solution)/shard_map/pallas_call | solution.py:454
  95.2 0.9 copy.8
  96.1 0.9 copy.9
where the time goes:
time: 97.2 us; the launch traced here: 97 us
  Pallas kernels  94.6 us (97%)
  local copies, waits for them, and re-layouts  1.81 us (2%)
    pallas_call x1, Pallas kernels, fused_body(): pl.pallas_call(fused_kernel, out_shape=(jax.ShapeDtypeStruct((rows, width...  94.6 us

commit v1 on v0

--- a/solution.py
+++ b/solution.py
@@ -142,10 +142,54 @@
     return jnp.where(position < length // 2, 2 * position, 2 * (length - 1 - position) + 1)
 
 
+GATE = 1
+PIECE = 256
+FORWARD_OP, CONTEXT_OP, MIX_OP, INPUT_OP, COT_GRAD_OP, NORM_GRAD_OP, ARRIVAL_OP = range(7)
+SLOT = 1024
+OP_SIZE = 128
+
+
+def schedules(images, pieces):
+    def context(b):
+        return [(CONTEXT_OP, c) for c in range(b * pieces, (b + 1) * pieces)]
+
+    def inputs(b):
+        return [(INPUT_OP, c) for c in range(b * pieces, (b + 1) * pieces)]
+
+    def each(op):
+        return [(op, b) for b in range(images)]
+
+    arrival, end = [(ARRIVAL_OP, 0)], images - 1
+    mixed = [step for b in range(images) for step in context(b) + [(MIX_OP, b)]]
+    sent = [step for b in range(images) for step in inputs(b)]
+    early = mixed + arrival + sent + each(FORWARD_OP) + each(COT_GRAD_OP) + each(NORM_GRAD_OP)
+    middle = arrival + each(FORWARD_OP) + context(0)
+    final = arrival + each(FORWARD_OP) + context(0)
+    kept = []
+    for b in range(end):
+        later = context(b + 1)
+        middle += [(MIX_OP, b)] + inputs(b) + [(COT_GRAD_OP, b)] + later[:-1]
+        middle += [(NORM_GRAD_OP, b)] + later[-1:]
+        final += [(COT_GRAD_OP, b), (MIX_OP, b), (NORM_GRAD_OP, b)] + later
+        kept += inputs(b)
+    middle += [(COT_GRAD_OP, end), (MIX_OP, end)] + inputs(end) + [(NORM_GRAD_OP, end)]
+    final += [(COT_GRAD_OP, end), (MIX_OP, end), (NORM_GRAD_OP, end)] + kept + inputs(end)
+    return early, middle, final
+
+
+def packed(steps):
+    codes = [op * OP_SIZE + argument for op, argument in steps]
+    codes += [0] * (-len(codes) % 3)
+    return [
+        codes[i] + codes[i + 1] * SLOT + codes[i + 2] * SLOT * SLOT
+        for i in range(0, len(codes), 3)
+    ]
+
+
 def fused_kernel(
     x_hbm, w_hbm, mix_hbm, oc_hbm, sc_hbm, wg_hbm,
     x_ref, mix_ref, sc_ref, wg_ref, sums, weights, scaled, inverse, normed, lefts, rights, mix_t, cot, d_ctx, vals, partial, landing,
-    ag_send, ag_recv, rs_send, rs_recv, cot_send, cot_recv, load_sem, sc_sem, wg_sem,
+    ag_send, ag_recv, rs_send, rs_recv, cot_send, cot_recv, load_sem, sc_sem, wg_sem, go_sem,
 ):
     n = lax.axis_size("dp")
     sections = lax.axis_size("pipe")
@@ -158,11 +202,15 @@
     width, both = weights.shape
     hd = both // 2
     images, heads, patches = mix_ref.shape[:3]
+    pieces = patches // PIECE
+    hops = n // 2
     tiles = hd // LANES
     near = (tiles + 1) // 2 * LANES
     far = hd - near
 
     last = s == sections - 1
+    leads = lax.rem(s, 2) == 1
+    partner = jnp.where(leads, s - 1, s + 1)
 
     def rows_of(position):
         return pl.ds(pl.multiple_of(ring_index(position, n) * share, 16), share)
@@ -182,28 +230,31 @@
         )
     pl.semaphore_wait(barrier, 4)
 
-    ag_streams = []
-    for direction, first, count in (
-        (1, hd, near), (-1, hd + near, far), (1, 0, far), (-1, far, near)
-    ):
-        cut = (count // LANES + 1) // 2 * LANES
-        ag_streams += [(direction, first, cut), (direction, first + cut, count - cut)]
-    lanes_of = range(len(ag_streams))
+    def tell_partner():
+        pl.semaphore_signal(go_sem, inc=1, device_id={"pipe": partner}, device_id_type=MESH)
+
+    streams = []
+    for half in (1, 0):
+        for first, count in ((0, near), (near, far)):
+            for direction in (1, -1):
+                whole = (first == 0) == ((direction == 1) == (half == 1))
+                streams.append((direction, half, first, count, whole))
+    lanes_of = range(len(streams))
+    output_lanes, value_lanes = lanes_of[:4], lanes_of[4:]
 
     def ag_copy(k, t, arriving):
-        direction, first, count = ag_streams[k]
+        direction, half, first, count, _ = streams[k]
         offset = t + 1 if arriving else t
         position = lax.rem(place - direction * offset + 2 * n, n)
-        block = weights.at[rows_of(position), pl.ds(first, count)]
+        block = weights.at[rows_of(position), pl.ds(half * hd + first, count)]
         return pltpu.make_async_remote_copy(
             src_ref=block, dst_ref=block,
             send_sem=ag_send.at[k, t], recv_sem=ag_recv.at[k, t],
             device_id={"dp": up if direction == 1 else down}, device_id_type=MESH,
         )
 
-    load_w.wait()
-    for k in lanes_of:
-        ag_copy(k, 0, False).start()
+    def travels(k, t):
+        return t < (hops if streams[k][4] else hops - 1)
 
     load_x.start()
     load_mix.start()
@@ -211,6 +262,15 @@
     @pl.when(last)
     def _():
         load_cot.start()
+
+    load_w.wait()
+
+    @pl.when(jnp.logical_not(leads))
+    def _():
+        pl.semaphore_wait(go_sem, 1)
+
+    for k in lanes_of:
+        ag_copy(k, 0, False).start()
 
     def prepare_rows(u):
         rows = pl.ds(pl.multiple_of(u * LANES, LANES), LANES)
@@ -230,7 +290,7 @@
 
     def prepare(t):
         for count, work in ((x_ref.shape[0] // LANES, prepare_rows), (images * heads, prepare_mix)):
-            pl.loop(t * count // (n - 1), (t + 1) * count // (n - 1))(work)
+            pl.loop(t * count // (hops - 1), (t + 1) * count // (hops - 1))(work)
 
     load_x.wait()
     load_mix.wait()
@@ -239,21 +299,27 @@
     def _():
         load_cot.wait()
 
-    @pl.loop(0, n - 1)
+    @pl.loop(0, hops - 1)
     def _(t):
         for k in lanes_of:
             ag_copy(k, t, True).wait_recv()
 
-            @pl.when(t < n - 2)
+            @pl.when(travels(k, t + 1))
             def _():
                 ag_copy(k, t + 1, False).start()
 
+        @pl.when(jnp.logical_and(leads, t == GATE))
+        def _():
+            tell_partner()
+
         prepare(t)
 
-    @pl.loop(0, n - 1)
-    def _(t):
-        for k in lanes_of:
-            ag_copy(k, t, False).wait_send()
+    def arrive(lanes):
+        for k in lanes:
+            if streams[k][4]:
+                ag_copy(k, hops - 1, True).wait_recv()
+
+    arrive(output_lanes)
 
     head_width = hd // heads
     lane = lax.broadcasted_iota(jnp.int32, (patches, LANES), 1)
@@ -274,41 +340,50 @@
                 if (h + 1) * head_width >= (tile + 1) * LANES:
                     dest[rows, tile * LANES : (tile + 1) * LANES] = made[tile].astype(jnp.bfloat16)
 
-    def cot_copy(b):
-        rows = pl.ds(pl.multiple_of(b * patches, patches), patches)
+    def image_rows(b):
+        return pl.ds(pl.multiple_of(b * patches, patches), patches)
+
+    def piece_rows(c):
+        return pl.ds(pl.multiple_of(c * PIECE, PIECE), PIECE)
+
+    def cot_copy(c):
+        rows = piece_rows(c)
         return pltpu.make_async_remote_copy(
             src_ref=sc_ref.at[rows, :], dst_ref=cot.at[rows, :],
-            send_sem=cot_send.at[b], recv_sem=cot_recv.at[b],
+            send_sem=cot_send.at[c], recv_sem=cot_recv.at[c],
             device_id={"pipe": lax.rem(s + sections - 1, sections)}, device_id_type=MESH,
         )
 
     d_values, context = rights.at[0], rights.at[1]
 
-    def sc_copy(b):
-        rows = pl.ds(pl.multiple_of(b * patches, patches), patches)
-        return pltpu.make_async_copy(sc_ref.at[rows, :], sc_hbm.at[rows, :], sc_sem.at[b])
+    def sc_copy(c):
+        rows = piece_rows(c)
+        return pltpu.make_async_copy(sc_ref.at[rows, :], sc_hbm.at[rows, :], sc_sem.at[c])
 
     def forward(b):
-        rows = pl.ds(pl.multiple_of(b * patches, patches), patches)
+        rows = image_rows(b)
         vals[rows, :] = jnp.dot(
             normed[rows, :], weights[:, :hd], preferred_element_type=jnp.float32
         ).astype(jnp.bfloat16)
         mix_rows(mix_ref, b, vals, context, rows)
 
-    def to_values(b):
-        rows = pl.ds(pl.multiple_of(b * patches, patches), patches)
+    def to_context(c):
+        rows = piece_rows(c)
 
         @pl.when(jnp.logical_not(last))
         def _():
-            cot_copy(b).wait_recv()
+            cot_copy(c).wait_recv()
 
         d_ctx[rows, :] = jnp.dot(
             cot[rows, :], weights[:, hd:], preferred_element_type=jnp.float32
         ).astype(jnp.bfloat16)
-        mix_rows(mix_t, b, d_ctx, d_values, rows)
-
-    def to_input(b):
-        rows = pl.ds(pl.multiple_of(b * patches, patches), patches)
+        lefts[1, :, rows] = cot[rows, :].T
+
+    def to_values(b):
+        mix_rows(mix_t, b, d_ctx, d_values, image_rows(b))
+
+    def to_input(c):
+        rows = piece_rows(c)
         d_normed = lax.dot_general(
             d_values[rows, :], weights[:, :hd], (((1,), (1,)), ((), ())),
             preferred_element_type=jnp.float32,
@@ -323,47 +398,51 @@
 
         @pl.when(s > 0)
         def _():
-            cot_copy(b).start()
-
-        sc_copy(b).start()
-
-    rs_streams = []
-    for direction, half, first, count in (
-        (1, 0, 0, near), (-1, 1, 0, near), (1, 0, near, far), (-1, 1, near, far)
-    ):
-        cut = (count // LANES + 1) // 2 * LANES
-        rs_streams += [
-            (direction, half, first, cut), (direction, half, first + cut, count - cut)
-        ]
+            cot_copy(c).start()
+
+        sc_copy(c).start()
+
+    def arrival(_):
+        arrive(value_lanes)
+
+        @pl.when(jnp.logical_not(leads))
+        def _():
+            tell_partner()
 
     def wg_copy(k):
-        _, half, first, count = rs_streams[k]
+        _, half, first, count, _ = streams[k]
         columns = pl.ds(half * hd + first, count)
         return pltpu.make_async_copy(wg_ref.at[:, columns], wg_hbm.at[:, columns], wg_sem.at[k])
 
-    def rs_copy(k, t):
-        direction, half, first, count = rs_streams[k]
+    def ahead(direction, distance):
+        return rows_of(lax.rem(place + direction * distance + n, n))
+
+    def rs_copy(k, t, first_leg=False):
+        direction, half, first, count, _ = streams[k]
         columns = pl.ds(first, count)
-        if isinstance(t, int):
-            origin = partial.at[half, rows_of(lax.rem(place - direction + n, n)), columns]
+        side = (1 - direction) // 2
+        if first_leg:
+            origin = partial.at[half, ahead(direction, hops - t), columns]
         else:
-            origin = landing.at[half, jnp.maximum(t - 1, 0), :, columns]
+            origin = landing.at[side, half, jnp.maximum(t - 1, 0), :, columns]
         return pltpu.make_async_remote_copy(
-            src_ref=origin, dst_ref=landing.at[half, t, :, columns],
+            src_ref=origin, dst_ref=landing.at[side, half, t, :, columns],
             send_sem=rs_send.at[k, t], recv_sem=rs_recv.at[k, t],
             device_id={"dp": up if direction == 1 else down}, device_id_type=MESH,
         )
 
+    def send_partials(lanes):
+        for k in sorted(lanes, key=lambda k: not streams[k][4]):
+            rs_copy(k, 0 if streams[k][4] else 1, True).start()
+
     part = width // 2
 
-    def gradients(b):
-        rows = pl.ds(pl.multiple_of(b * patches, patches), patches)
-        lefts[1, :, rows] = cot[rows, :].T
-
-        @pl.loop(0, 4)
+    def gradients(half, b):
+        rows = image_rows(b)
+
+        @pl.loop(0, 2)
         def _(i):
-            half = i // 2
-            block = pl.ds(pl.multiple_of(lax.rem(i, 2) * part, 16), part)
+            block = pl.ds(pl.multiple_of(i * part, 16), part)
             term = jnp.dot(
                 lefts[half, block, rows], rights[half, rows, :],
                 preferred_element_type=jnp.float32,
@@ -382,64 +461,89 @@
                 total = term if images == 1 else sums[half, block, :] + term
                 partial[half, block, :] = total.astype(jnp.bfloat16)
 
+    def cot_gradient(b):
+        gradients(1, b)
+
         @pl.when(b == images - 1)
         def _():
-            for k in lanes_of:
-                rs_copy(k, 0).start()
-
-    @pl.loop(0, 4 * images)
+            @pl.when(leads)
+            def _():
+                pl.semaphore_wait(go_sem, 1)
+
+            send_partials(output_lanes)
+
+    def norm_gradient(b):
+        gradients(0, b)
+
+        @pl.when(b == images - 1)
+        def _():
+            send_partials(value_lanes)
+
+    early, middle, final = (packed(steps) for steps in schedules(images, pieces))
+    words = [
+        jnp.where(s == 0, c, jnp.where(jnp.logical_and(leads, jnp.logical_not(last)), b, a))
+        for a, b, c in zip(early, middle, final)
+    ]
+    actions = (forward, to_context, to_values, to_input, cot_gradient, norm_gradient, arrival)
+
+    @pl.loop(0, len(schedules(images, pieces)[0]))
     def _(i):
-        early = i < images
-        after = jnp.maximum(i - images, 0)
-        turn = lax.rem(after, 3)
-        own = jnp.where(early, 0, jnp.where(s == 0, jnp.where(turn == 0, 1, 4 - turn), 1 + turn))
-        own_b = jnp.where(early, i, after // 3)
-        final = jnp.where(
-            i < 2 * images, 1 + lax.rem(i, 2), jnp.where(i < 3 * images, 0, 3)
-        )
-        final_b = jnp.where(i < 2 * images, i // 2, lax.rem(i, images))
-        work = jnp.where(last, final, own)
-        b = jnp.where(last, final_b, own_b)
-        for number, action in enumerate((forward, to_values, to_input, gradients)):
-            pl.when(work == number)(functools.partial(action, b))
-
-    @pl.loop(0, n - 1)
+        group, slot = i // 3, lax.rem(i, 3)
+        word = words[0]
+        for j in range(1, len(words)):
+            word = jnp.where(group == j, words[j], word)
+        code = jnp.where(slot == 0, word, jnp.where(slot == 1, word // SLOT, word // (SLOT * SLOT)))
+        code = lax.rem(code, SLOT)
+        work, argument = code // OP_SIZE, lax.rem(code, OP_SIZE)
+        for number, action in enumerate(actions):
+            pl.when(work == number)(functools.partial(action, argument))
+
+    @pl.loop(1, hops)
+    def _(t):
+        def add_on(k):
+            direction, half, first, count, _ = streams[k]
+            columns = pl.ds(first, count)
+            side = (1 - direction) // 2
+            rs_copy(k, t - 1).wait_recv()
+            total = landing[side, half, t - 1, :, columns].astype(jnp.float32) + partial[
+                half, ahead(direction, hops - t), columns
+            ].astype(jnp.float32)
+            landing[side, half, t - 1, :, columns] = total.astype(jnp.bfloat16)
+            rs_copy(k, t).start()
+
+        for k in lanes_of:
+            if streams[k][4]:
+                add_on(k)
+            else:
+                pl.when(t > 1)(functools.partial(add_on, k))
+
+    for k in lanes_of[::2]:
+        _, half, first, count, _ = streams[k]
+        columns = pl.ds(first, count)
+        total = partial[half, rows_of(place), columns].astype(jnp.float32)
+        for side in range(2):
+            rs_copy(k + side, hops - 1).wait_recv()
+            total += landing[side, half, hops - 1, :, columns].astype(jnp.float32)
+        wg_ref[:, pl.ds(half * hd + first, count)] = total
+        wg_copy(k).start()
+
+    @pl.loop(0, hops)
     def _(t):
         for k in lanes_of:
-            direction, half, first, count = rs_streams[k]
-            columns = pl.ds(first, count)
-            rs_copy(k, t).wait_recv()
-            position = lax.rem(place - direction * (t + 2) + 2 * n, n)
-            total = landing[half, t, :, columns].astype(jnp.float32) + partial[
-                half, rows_of(position), columns
-            ].astype(jnp.float32)
-
-            @pl.when(t < n - 2)
-            def _():
-                landing[half, t, :, columns] = total.astype(jnp.bfloat16)
-                rs_copy(k, t + 1).start()
-
-            @pl.when(t == n - 2)
-            def _():
-                wg_ref[:, pl.ds(half * hd + first, count)] = total
-                wg_copy(k).start()
-
-    @pl.loop(0, n - 1)
-    def _(t):
-        for k in lanes_of:
-            rs_copy(k, t).wait_send()
+            pl.when(travels(k, t))(lambda: ag_copy(k, t, False).wait_send())
+            pl.when(travels(k, hops - 1 - t))(lambda: rs_copy(k, t).wait_send())
 
     @pl.when(s > 0)
     def _():
-        @pl.loop(0, images)
-        def _(b):
-            cot_copy(b).wait_send()
-
-    @pl.loop(0, images)
-    def _(b):
-        sc_copy(b).wait()
-
-    for k in lanes_of:
+        @pl.loop(0, images * pieces)
+        def _(c):
+            cot_copy(c).wait_send()
+
+    @pl.loop(0, images * pieces)
+    def _(c):
+        sc_copy(c).wait()
+
+    for k in lanes_of[::2]:
         wg_copy(k).wait()
 
 
@@ -476,16 +580,17 @@
             pltpu.VMEM((rows, hd), bf16),
             pltpu.VMEM((rows, hd), bf16),
             pltpu.VMEM((2, width, hd), bf16),
-            pltpu.VMEM((2, n - 1, share, hd), bf16),
-            pltpu.SemaphoreType.DMA((8, n - 1)),
-            pltpu.SemaphoreType.DMA((8, n - 1)),
-            pltpu.SemaphoreType.DMA((8, n - 1)),
-            pltpu.SemaphoreType.DMA((8, n - 1)),
-            pltpu.SemaphoreType.DMA((images,)),
-            pltpu.SemaphoreType.DMA((images,)),
+            pltpu.VMEM((2, 2, n // 2, share, hd), bf16),
+            pltpu.SemaphoreType.DMA((8, n // 2)),
+            pltpu.SemaphoreType.DMA((8, n // 2)),
+            pltpu.SemaphoreType.DMA((8, n // 2)),
+            pltpu.SemaphoreType.DMA((8, n // 2)),
+            pltpu.SemaphoreType.DMA((rows // LANES,)),
+            pltpu.SemaphoreType.DMA((rows // LANES,)),
             pltpu.SemaphoreType.DMA((4,)),
-            pltpu.SemaphoreType.DMA((images,)),
+            pltpu.SemaphoreType.DMA((rows // LANES,)),
             pltpu.SemaphoreType.DMA((8,)),
+            pltpu.SemaphoreType.REGULAR,
         ],
         compiler_params=pltpu.CompilerParams(
             collective_id=0, has_side_effects=True, vmem_limit_bytes=48 * 1024 * 1024
@@ -502,10 +607,12 @@
         share % 16 == 0
         and both % (2 * LANES) == 0
         and width % LANES == 0
-        and mixing.shape[3] % LANES == 0
+        and mixing.shape[3] % PIECE == 0
         and n % 2 == 0
+        and n > 2
         and lax.axis_size("pipe") > 2
         and lax.axis_size("pipe") % 2 == 0
+        and out_cotangent.shape[0] < OP_SIZE * LANES
     )
     chosen = fused_body if aligned else body
     return chosen(saved_inputs, projections, mixing, out_cotangent)

time: 97.2 us -> 90.4 us (0.930)
  Pallas kernels: 94.6 us -> 87.8 us
    pallas_call x1, Pallas kernels: 94.6 us -> 87.8 us  [fused_body(): pl.pallas_call(fused_kernel, out_shape=(jax.ShapeDtypeStruct((rows, width...]
where the time goes in v1:
time: 90.4 us; the launch traced here: 90.3 us
  Pallas kernels  87.8 us (97%)
  local copies, waits for them, and re-layouts  1.81 us (2%)
    pallas_call x1, Pallas kernels, fused_body(): pl.pallas_call(fused_kernel, out_shape=(jax.ShapeDtypeStruct((rows, width...  87.8 us
    unnamed x2, local copies, waits for them, and re-layouts  1.81 us

profile of v1, /device:TPU:0, one launch (start us, length us, event | category | flops | bytes accessed | tf_op | source)
XLA Modules:
  0.0 90.3 jit_solution(11986125749000352471)
XLA Ops:
  0.6 87.8 %shard_map.59 = (bf16[512,896]{1,0:T(8,128)(2,1)S(1)}, f32[112,1792]{1,0:T(8,128)S(1)}) custom-call(bf16[512,896]{1,0:T(8,128)(2,1)} %bitcast.8, bf16[112,1792]{1,0:T(8,128)(2,1)} %bitcast.9, bf16[2,8,256,256]{3,2,1,0:T(8,128)(2,1)} %bitcast.7, bf16[512,896]{1,0:T(8,128)(2,1)} %oc_hbm.1), custom_call_target="tpu_custom_call" | custom-call | tf_op jit(solution)/shard_map/pallas_call | solution.py:558
  88.5 0.9 %copy.8 = bf16[1,512,896]{2,1,0:T(8,128)(2,1)} copy(bf16[1,512,896]{2,1,0:T(8,128)(2,1)S(1)} %bitcast.5) | data formatting | bytes 1835008
  89.4 0.9 copy.9

commit v2 on v1

--- a/solution.py
+++ b/solution.py
@@ -142,38 +142,29 @@
     return jnp.where(position < length // 2, 2 * position, 2 * (length - 1 - position) + 1)
 
 
-GATE = 1
-PIECE = 256
-FORWARD_OP, CONTEXT_OP, MIX_OP, INPUT_OP, COT_GRAD_OP, NORM_GRAD_OP, ARRIVAL_OP = range(7)
+GATE = 0
+FORWARD_OP, CONTEXT_OP, MIX_OP, INPUT_OP, COT_GRAD_OP, NORM_GRAD_OP, ARRIVAL_OP, RECEIVE_OP = range(8)
 SLOT = 1024
 OP_SIZE = 128
 
 
-def schedules(images, pieces):
-    def context(b):
-        return [(CONTEXT_OP, c) for c in range(b * pieces, (b + 1) * pieces)]
-
-    def inputs(b):
-        return [(INPUT_OP, c) for c in range(b * pieces, (b + 1) * pieces)]
-
-    def each(op):
-        return [(op, b) for b in range(images)]
+def schedules(images):
+    def each(*ops):
+        return [(op, b) for b in range(images) for op in ops]
 
     arrival, end = [(ARRIVAL_OP, 0)], images - 1
-    mixed = [step for b in range(images) for step in context(b) + [(MIX_OP, b)]]
-    sent = [step for b in range(images) for step in inputs(b)]
-    early = mixed + arrival + sent + each(FORWARD_OP) + each(COT_GRAD_OP) + each(NORM_GRAD_OP)
-    middle = arrival + each(FORWARD_OP) + context(0)
-    final = arrival + each(FORWARD_OP) + context(0)
-    kept = []
+    early = [(op, 0) for op in (RECEIVE_OP, CONTEXT_OP, MIX_OP)] + arrival + [(INPUT_OP, 0)]
+    for b in range(1, images):
+        early += [(op, b) for op in (RECEIVE_OP, CONTEXT_OP, MIX_OP, INPUT_OP)]
+    early += each(FORWARD_OP) + each(COT_GRAD_OP) + each(NORM_GRAD_OP)
+    middle = arrival + each(FORWARD_OP)
     for b in range(end):
-        later = context(b + 1)
-        middle += [(MIX_OP, b)] + inputs(b) + [(COT_GRAD_OP, b)] + later[:-1]
-        middle += [(NORM_GRAD_OP, b)] + later[-1:]
-        final += [(COT_GRAD_OP, b), (MIX_OP, b), (NORM_GRAD_OP, b)] + later
-        kept += inputs(b)
-    middle += [(COT_GRAD_OP, end), (MIX_OP, end)] + inputs(end) + [(NORM_GRAD_OP, end)]
-    final += [(COT_GRAD_OP, end), (MIX_OP, end), (NORM_GRAD_OP, end)] + kept + inputs(end)
+        middle += [(op, b) for op in (RECEIVE_OP, CONTEXT_OP, MIX_OP, INPUT_OP, COT_GRAD_OP, NORM_GRAD_OP)]
+    middle += [
+        (op, end) for op in (RECEIVE_OP, COT_GRAD_OP, CONTEXT_OP, MIX_OP, INPUT_OP, NORM_GRAD_OP)
+    ]
+    final = arrival + each(FORWARD_OP)
+    final += each(RECEIVE_OP, COT_GRAD_OP, CONTEXT_OP, MIX_OP, NORM_GRAD_OP) + each(INPUT_OP)
     return early, middle, final
 
 
@@ -188,8 +179,8 @@
 
 def fused_kernel(
     x_hbm, w_hbm, mix_hbm, oc_hbm, sc_hbm, wg_hbm,
-    x_ref, mix_ref, sc_ref, wg_ref, sums, weights, scaled, inverse, normed, lefts, rights, mix_t, cot, d_ctx, vals, partial, landing,
-    ag_send, ag_recv, rs_send, rs_recv, cot_send, cot_recv, load_sem, sc_sem, wg_sem, go_sem,
+    x_ref, mix_ref, sc_ref, wg_ref, sums, weights, extra, scaled, inverse, normed, lefts, rights, mix_t, cot, d_ctx, vals, partial, landing,
+    ag_send, ag_recv, rs_send, rs_recv, cot_send, cot_recv, load_sem, sc_sem, wg_sem, seed_send, seed_recv, ring_send, ring_recv, back_send, back_recv, go_sem,
 ):
     n = lax.axis_size("dp")
     sections = lax.axis_size("pipe")
@@ -202,7 +193,6 @@
     width, both = weights.shape
     hd = both // 2
     images, heads, patches = mix_ref.shape[:3]
-    pieces = patches // PIECE
     hops = n // 2
     tiles = hd // LANES
     near = (tiles + 1) // 2 * LANES
@@ -211,6 +201,9 @@
     last = s == sections - 1
     leads = lax.rem(s, 2) == 1
     partner = jnp.where(leads, s - 1, s + 1)
+    helped = s == sections - 2
+    helps = s == sections - 4
+    alone = jnp.logical_not(helped)
 
     def rows_of(position):
         return pl.ds(pl.multiple_of(ring_index(position, n) * share, 16), share)
@@ -224,11 +217,12 @@
     barrier = pltpu.get_barrier_semaphore()
     for target in ({"dp": up}, {"dp": down}):
         pl.semaphore_signal(barrier, inc=1, device_id=target, device_id_type=MESH)
-    for step in (1, sections - 1):
+    steps = sorted({1, 2, sections - 2, sections - 1})
+    for step in steps:
         pl.semaphore_signal(
             barrier, inc=1, device_id={"pipe": lax.rem(s + step, sections)}, device_id_type=MESH
         )
-    pl.semaphore_wait(barrier, 4)
+    pl.semaphore_wait(barrier, 2 + len(steps))
 
     def tell_partner():
         pl.semaphore_signal(go_sem, inc=1, device_id={"pipe": partner}, device_id_type=MESH)
@@ -263,14 +257,81 @@
     def _():
         load_cot.start()
 
+    def ring_copy(k, t, arriving):
+        direction, _, first, count, _ = streams[k]
+        offset = t + 1 if arriving else t
+        position = lax.rem(place - direction * offset + 2 * n, n)
+        block = extra.at[rows_of(position), pl.ds(first, count)]
+        return pltpu.make_async_remote_copy(
+            src_ref=block, dst_ref=block,
+            send_sem=ring_send.at[k - 4, t], recv_sem=ring_recv.at[k - 4, t],
+            device_id={"dp": up if direction == 1 else down}, device_id_type=MESH,
+        )
+
+    def back_copy(k, t):
+        direction, _, first, count, _ = streams[k]
+        rows = rows_of(lax.rem(place - direction * (t + 1) + 2 * n, n))
+        columns = pl.ds(first, count)
+        return pltpu.make_async_remote_copy(
+            src_ref=extra.at[rows, columns], dst_ref=weights.at[rows, columns],
+            send_sem=back_send.at[k - 4, t], recv_sem=back_recv.at[k - 4, t],
+            device_id={"pipe": lax.rem(s + 2, sections)}, device_id_type=MESH,
+        )
+
+    def seed_copy(k):
+        _, _, first, count, _ = streams[k]
+        rows, columns = rows_of(place), pl.ds(first, count)
+        return pltpu.make_async_remote_copy(
+            src_ref=weights.at[rows, columns], dst_ref=extra.at[rows, columns],
+            send_sem=seed_send.at[k // 2 - 2], recv_sem=seed_recv.at[k // 2 - 2],
+            device_id={"pipe": lax.rem(s + sections - 2, sections)}, device_id_type=MESH,
+        )
+
+    def relay(k, t):
+        ring_copy(k, t, True).wait_recv()
+
+        @pl.when(travels(k, t + 1))
+        def _():
+            ring_copy(k, t + 1, False).start()
+
+        back_copy(k, t).start()
+
     load_w.wait()
 
+    @pl.when(helped)
+    def _():
+        for k in value_lanes[::2]:
+            seed_copy(k).start()
+
+    @pl.when(helps)
+    def _():
+        for k in value_lanes[::2]:
+            seed_copy(k).wait_recv()
+            for side in range(2):
+                ring_copy(k + side, 0, False).start()
+
+        @pl.loop(0, hops - 1)
+        def _(t):
+            for k in value_lanes:
+                relay(k, t)
+
     @pl.when(jnp.logical_not(leads))
     def _():
         pl.semaphore_wait(go_sem, 1)
 
-    for k in lanes_of:
+    for k in output_lanes:
         ag_copy(k, 0, False).start()
+
+    @pl.when(alone)
+    def _():
+        for k in value_lanes:
+            ag_copy(k, 0, False).start()
+
+    @pl.when(helps)
+    def _():
+        for k in value_lanes:
+            if streams[k][4]:
+                relay(k, hops - 1)
 
     def prepare_rows(u):
         rows = pl.ds(pl.multiple_of(u * LANES, LANES), LANES)
@@ -299,14 +360,22 @@
     def _():
         load_cot.wait()
 
+    def pass_on(k, t):
+        ag_copy(k, t, True).wait_recv()
+
+        @pl.when(travels(k, t + 1))
+        def _():
+            ag_copy(k, t + 1, False).start()
+
     @pl.loop(0, hops - 1)
     def _(t):
-        for k in lanes_of:
-            ag_copy(k, t, True).wait_recv()
-
-            @pl.when(travels(k, t + 1))
-            def _():
-                ag_copy(k, t + 1, False).start()
+        for k in output_lanes:
+            pass_on(k, t)
+
+        @pl.when(alone)
+        def _():
+            for k in value_lanes:
+                pass_on(k, t)
 
         @pl.when(jnp.logical_and(leads, t == GATE))
         def _():
@@ -343,11 +412,8 @@
     def image_rows(b):
         return pl.ds(pl.multiple_of(b * patches, patches), patches)
 
-    def piece_rows(c):
-        return pl.ds(pl.multiple_of(c * PIECE, PIECE), PIECE)
-
     def cot_copy(c):
-        rows = piece_rows(c)
+        rows = image_rows(c)
         return pltpu.make_async_remote_copy(
             src_ref=sc_ref.at[rows, :], dst_ref=cot.at[rows, :],
             send_sem=cot_send.at[c], recv_sem=cot_recv.at[c],
@@ -357,7 +423,7 @@
     d_values, context = rights.at[0], rights.at[1]
 
     def sc_copy(c):
-        rows = piece_rows(c)
+        rows = image_rows(c)
         return pltpu.make_async_copy(sc_ref.at[rows, :], sc_hbm.at[rows, :], sc_sem.at[c])
 
     def forward(b):
@@ -367,23 +433,26 @@
         ).astype(jnp.bfloat16)
         mix_rows(mix_ref, b, vals, context, rows)
 
+    def receive(c):
+        rows = image_rows(c)
+
+        @pl.when(jnp.logical_not(last))
+        def _():
+            cot_copy(c).wait_recv()
+
+        lefts[1, :, rows] = cot[rows, :].T
+
     def to_context(c):
-        rows = piece_rows(c)
-
-        @pl.when(jnp.logical_not(last))
-        def _():
-            cot_copy(c).wait_recv()
-
+        rows = image_rows(c)
         d_ctx[rows, :] = jnp.dot(
             cot[rows, :], weights[:, hd:], preferred_element_type=jnp.float32
         ).astype(jnp.bfloat16)
-        lefts[1, :, rows] = cot[rows, :].T
 
     def to_values(b):
         mix_rows(mix_t, b, d_ctx, d_values, image_rows(b))
 
     def to_input(c):
-        rows = piece_rows(c)
+        rows = image_rows(c)
         d_normed = lax.dot_general(
             d_values[rows, :], weights[:, :hd], (((1,), (1,)), ((), ())),
             preferred_element_type=jnp.float32,
@@ -403,7 +472,14 @@
         sc_copy(c).start()
 
     def arrival(_):
-        arrive(value_lanes)
+        pl.when(alone)(functools.partial(arrive, value_lanes))
+
+        @pl.when(helped)
+        def _():
+            @pl.loop(0, hops)
+            def _(t):
+                for k in value_lanes:
+                    pl.when(travels(k, t))(lambda: back_copy(k, t).wait_recv())
 
         @pl.when(jnp.logical_not(leads))
         def _():
@@ -479,14 +555,14 @@
         def _():
             send_partials(value_lanes)
 
-    early, middle, final = (packed(steps) for steps in schedules(images, pieces))
+    early, middle, final = (packed(steps) for steps in schedules(images))
     words = [
         jnp.where(s == 0, c, jnp.where(jnp.logical_and(leads, jnp.logical_not(last)), b, a))
         for a, b, c in zip(early, middle, final)
     ]
-    actions = (forward, to_context, to_values, to_input, cot_gradient, norm_gradient, arrival)
-
-    @pl.loop(0, len(schedules(images, pieces)[0]))
+    actions = (forward, to_context, to_values, to_input, cot_gradient, norm_gradient, arrival, receive)
+
+    @pl.loop(0, len(schedules(images)[0]))
     def _(i):
         group, slot = i // 3, lax.rem(i, 3)
         word = words[0]
@@ -530,16 +606,32 @@
     @pl.loop(0, hops)
     def _(t):
         for k in lanes_of:
-            pl.when(travels(k, t))(lambda: ag_copy(k, t, False).wait_send())
+            sent = travels(k, t) if k in output_lanes else jnp.logical_and(alone, travels(k, t))
+            pl.when(sent)(lambda: ag_copy(k, t, False).wait_send())
             pl.when(travels(k, hops - 1 - t))(lambda: rs_copy(k, t).wait_send())
 
+    @pl.when(helped)
+    def _():
+        for k in value_lanes[::2]:
+            seed_copy(k).wait_send()
+
+    @pl.when(helps)
+    def _():
+        @pl.loop(0, hops)
+        def _(t):
+            for k in value_lanes:
+                @pl.when(travels(k, t))
+                def _():
+                    ring_copy(k, t, False).wait_send()
+                    back_copy(k, t).wait_send()
+
     @pl.when(s > 0)
     def _():
-        @pl.loop(0, images * pieces)
+        @pl.loop(0, images)
         def _(c):
             cot_copy(c).wait_send()
 
-    @pl.loop(0, images * pieces)
+    @pl.loop(0, images)
     def _(c):
         sc_copy(c).wait()
 
@@ -570,6 +662,7 @@
             pltpu.VMEM((share, both), f32),
             pltpu.VMEM((2, width, hd), f32),
             pltpu.VMEM((width, both), bf16),
+            pltpu.VMEM((width, hd), bf16),
             pltpu.VMEM((rows, width), f32),
             pltpu.VMEM((rows, 1), f32),
             pltpu.VMEM((rows, width), bf16),
@@ -590,6 +683,12 @@
             pltpu.SemaphoreType.DMA((4,)),
             pltpu.SemaphoreType.DMA((rows // LANES,)),
             pltpu.SemaphoreType.DMA((8,)),
+            pltpu.SemaphoreType.DMA((2,)),
+            pltpu.SemaphoreType.DMA((2,)),
+            pltpu.SemaphoreType.DMA((4, n // 2)),
+            pltpu.SemaphoreType.DMA((4, n // 2)),
+            pltpu.SemaphoreType.DMA((4, n // 2)),
+            pltpu.SemaphoreType.DMA((4, n // 2)),
             pltpu.SemaphoreType.REGULAR,
         ],
         compiler_params=pltpu.CompilerParams(
@@ -607,7 +706,7 @@
         share % 16 == 0
         and both % (2 * LANES) == 0
         and width % LANES == 0
-        and mixing.shape[3] % PIECE == 0
+        and mixing.shape[3] % LANES == 0
         and n % 2 == 0
         and n > 2
         and lax.axis_size("pipe") > 2

time: 90.4 us -> 86.7 us (0.959)
  Pallas kernels: 87.8 us -> 84.1 us
    pallas_call x1, Pallas kernels: 87.8 us -> 84.1 us  [fused_body(): pl.pallas_call(fused_kernel, out_shape=(jax.ShapeDtypeStruct((rows, width...]
where the time goes in v2:
time: 86.7 us; the launch traced here: 86.6 us
  Pallas kernels  84.1 us (97%)
  local copies, waits for them, and re-layouts  1.81 us (2%)
    pallas_call x1, Pallas kernels, fused_body(): pl.pallas_call(fused_kernel, out_shape=(jax.ShapeDtypeStruct((rows, width...  84.1 us
    unnamed x2, local copies, waits for them, and re-layouts  1.81 us

profile of v2, /device:TPU:0, one launch (start us, length us, event | category | flops | bytes accessed | tf_op | source)
XLA Modules:
  0.0 86.6 jit_solution(14406209464613213665)
XLA Ops:
  0.6 84.1 %shard_map.59 = (bf16[512,896]{1,0:T(8,128)(2,1)S(1)}, f32[112,1792]{1,0:T(8,128)S(1)}) custom-call(bf16[512,896]{1,0:T(8,128)(2,1)} %bitcast.8, bf16[112,1792]{1,0:T(8,128)(2,1)} %bitcast.9, bf16[2,8,256,256]{3,2,1,0:T(8,128)(2,1)} %bitcast.7, bf16[512,896]{1,0:T(8,128)(2,1)} %oc_hbm.1), custom_call_target="tpu_custom_call" | custom-call | tf_op jit(solution)/shard_map/pallas_call | solution.py:650
  84.8 0.9 %copy.8 = bf16[1,512,896]{2,1,0:T(8,128)(2,1)} copy(bf16[1,512,896]{2,1,0:T(8,128)(2,1)S(1)} %bitcast.5) | data formatting | bytes 1835008
  85.7 0.9 %copy.9 = f32[1,112,1792]{2,1,0:T(8,128)} copy(f32[1,112,1792]{2,1,0:T(8,128)S(1)} %bitcast.6) | data formatting | bytes 1605632
